TPU v7x, 32 devices: a whole 2x2x4 slice. The times are simulated.
32 devices in a mesh: expert: 8 (over z, y), blk: 4 (over x, core).
Axes of the slice: x: 2, y: 2, z: 4, core: 2. Of those that a mesh axis runs over, the one named last changes fastest.
Arguments:
- inputs: bfloat16 [8, 768, 1536], P('expert', 'blk'), may hold values from -6 to 6
- output_grads: bfloat16 [8, 768, 4096], P('expert', 'blk'), may hold values from -0.21875 to 0.21875
- route_counts: int32 [8, 4], P('expert', 'blk'), may hold values from 48 to 192, as said below
- left_rows: bfloat16 [8, 2304, 1536], P(None, 'expert', 'blk'), as said below
- left_lengths: int32 [8, 8], replicated, may hold values from 96 to 288, as said below
- right_inverse: bfloat16 [8, 4096, 4096], P('expert', 'blk'), may hold values from -0.09375 to 0.09375
Outputs:
- preconditioned: float32 [8, 4096, 1536], P('expert', 'blk')
Inputs may be any that keep to these rules, and one draw needn't show every extreme that they name: `route_counts`: for every expert, one device of blk holds exactly 192 routed tokens and one holds exactly 48. `left_lengths`: each row sums to 1536; in each row one owner holds exactly 288 rows and one exactly 96. `left_rows`: slots i * 288 + j with j >= left_lengths[e, i] are zero.
All inputs are finite; a program needn't handle non-finite values.
Results may differ from a plain program's by a relative error of at most 0.0041.
Values may be sent and summed in bfloat16 or wider, within the bound.
A program may use at most 128 MiB of HBM per device.

v0:
```python
import jax
import jax.numpy as jnp
from jax import lax
from jax.sharding import PartitionSpec as P


def shards(inputs, output_grads, route_counts, left_rows, left_lengths, right_inverse):
    token_rows = inputs[0]
    grad_rows = output_grads[0]
    slot_count = token_rows.shape[0]
    width_in = token_rows.shape[1]
    live_rows = lax.broadcasted_iota(jnp.int32, (slot_count, 1), 0) < route_counts[0, 0]
    masked = jnp.where(live_rows, token_rows, jnp.zeros_like(token_rows))
    contract_rows = (((0,), (0,)), ((), ()))
    columns = lax.all_to_all(grad_rows, "blk", split_axis=1, concat_axis=0, tiled=True)
    gradient = lax.dot_general(
        columns,
        lax.all_gather(masked, "blk", axis=0, tiled=True),
        contract_rows,
        preferred_element_type=jnp.float32,
    )
    gradient = gradient.astype(jnp.bfloat16)
    own_expert = lax.axis_index("expert")
    lengths = lax.dynamic_index_in_dim(left_lengths, own_expert, 0, keepdims=False)
    starts = jnp.cumsum(lengths) - lengths
    owners = lengths.shape[0]
    piece_slots = left_rows.shape[1]
    offset = lax.broadcasted_iota(jnp.int32, (owners, piece_slots), 1)
    row_index = jnp.minimum(starts[:, None] + offset, width_in - 1).reshape(owners * piece_slots)
    kept_rows = (offset < lengths[:, None]).reshape(1, owners * piece_slots)
    picked = jnp.where(
        kept_rows, jnp.take(gradient, row_index, axis=1), jnp.zeros((), jnp.bfloat16)
    )
    arrived = lax.all_to_all(left_rows, "expert", split_axis=0, concat_axis=1, tiled=True)
    weighted = jnp.dot(
        picked,
        lax.all_gather(arrived, "blk", axis=2, tiled=True)[0],
        preferred_element_type=jnp.float32,
    ).astype(jnp.bfloat16)
    inverse_rows = right_inverse[0]
    everything = lax.all_gather(weighted, "blk", axis=0, tiled=True)
    result = jnp.dot(inverse_rows, everything, preferred_element_type=jnp.float32)
    return result[None]


def solution(mesh):
    in_specs = (
        P("expert", "blk", None),
        P("expert", "blk", None),
        P("expert", "blk"),
        P(None, "expert", "blk"),
        P(),
        P("expert", "blk", None),
    )
    out_specs = P("expert", "blk", None)
    return jax.shard_map(shards, mesh=mesh, in_specs=in_specs, out_specs=out_specs, check_vma=False)
```

profile of v0, /device:TPU:0, one launch (start us, length us, event | category | flops | bytes accessed | tf_op | source)
XLA Modules:
  0.0 251.2 jit_solution(289022120514469136)
XLA Ops:
  6.5 0.0 copy-start
  6.5 0.0 all-gather.4.cloned.1.call-start
  7.3 2.0 bitcast_select_fusion
  9.3 0.0 all-gather.4.cloned.1.call-update
  9.3 0.0 all-gather.6.cloned.1.call-start
  9.4 48.7 %all_to_all.31 = bf16[8,288,384]{2,1,0:T(8,128)(2,1)} all-to-all(bf16[8,288,384]{2,1,0:T(8,128)(2,1)} %param.9), channel_id=1, replica_groups=mesh['expert'=8,'blk'=4] {'expert'}, dimensions={0} | all-to-all | bytes 3538944 | tf_op jit(solution)/shard_map/all_to_all | solution.py:34
  58.1 0.0 all-gather.6.cloned.1.call-update
  58.1 0.0 copy-done
  58.1 1.2 all_to_all.23
  59.3 1.6 copy.11
  60.9 3.6 %all-to-all-start = ((bf16[192,4,1024]{2,0,1:T(8,128)(2,1)}), bf16[192,4,1024]{2,0,1:T(8,128)(2,1)S(1)}, u32[]{:S(2)}, u32[]{:S(2)}) async-start(bf16[192,4,1024]{2,0,1:T(8,128)(2,1)} %copy.11), calls=%async_computation | async-start | bytes 3145728 | tf_op jit(solution)/shard_map/all_to_all | solution.py:15
  64.5 0.0 all-gather.8.cloned.1.call-start
  64.6 0.7 fusion.20
  65.3 0.2 reduce-window.8
  65.5 0.7 bitcast_subtract_fusion
  66.2 0.1 add_minimum_fusion
  66.3 0.1 min.28
  66.3 0.1 min.26
  66.4 0.1 iota_compare_fusion
  66.5 0.1 lt.57
  66.7 34.6 %all-to-all-done = bf16[192,4,1024]{2,0,1:T(8,128)(2,1)S(1)} async-done(((bf16[192,4,1024]{2,0,1:T(8,128)(2,1)}), bf16[192,4,1024]{2,0,1:T(8,128)(2,1)S(1)}, u32[]{:S(2)}, u32[]{:S(2)}) %all-to-all-start) | async-done | bytes 1572896 | tf_op jit(solution)/shard_map/all_to_all | solution.py:15
  101.2 0.0 copy-start.1
  101.2 0.0 all-gather.4.cloned.1.call-done
  101.2 1.1 copy-done.1
  102.4 4.8 %fusion.16 = bf16[1024,1536]{0,1:T(8,128)(2,1)S(1)} fusion(bf16[768,1536]{1,0:T(8,128)(2,1)} %all-gather.4.cloned.1.call-done, bf16[768,1024]{1,0:T(8,128)(2,1)} %bitcast.35), kind=kOutput, calls=%fused_computation.12 | convolution fusion | flops 2417491968 | bytes 7077888 | tf_op jit(solution)/shard_map/dot_general | solution.py:16
  107.1 8.1 %gather_fusion = bf16[2304,1024]{1,0:T(8,128)(2,1)} fusion(bf16[1024,1536]{0,1:T(8,128)(2,1)S(1)} %fusion.16, s32[3072]{0:T(1024)S(1)} %pad_clamp_fusion), kind=kCustom, calls=%fused_computation | custom fusion | bytes 9446400 | tf_op jit(solution)/shard_map/jit(_take)/gather | solution.py:32
  115.2 8.9 %all-gather.6.cloned.1.call-done = bf16[1,2304,1536]{2,1,0:T(8,128)(2,1)} async-done(((bf16[1,2304,384]{2,1,0:T(8,128)(2,1)}), bf16[1,2304,1536]{2,1,0:T(8,128)(2,1)}) %all-gather.6.cloned.1.call-update) | async-done | bytes 7077904 | tf_op jit(solution)/shard_map/all_gather | solution.py:37
  124.1 14.1 %fusion.11 = bf16[1024,1536]{1,0:T(8,128)(2,1)} fusion(bf16[1,2304,1536]{2,1,0:T(8,128)(2,1)} %all-gather.6.cloned.1.call-done, bf16[2304,1024]{1,0:T(8,128)(2,1)} %gather_fusion, pred[2304]{0:T(1024)(128)(4,1)S(1)} %lt.57, pred[2304]{0:T(1024)(128)(4,1)S(1)} %compare_and_fusion), kind=kOutput, calls=%fused_computation.10 | convolution fusion | flops 7254048768 | bytes 14946816 | tf_op jit(solution)/shard_map/dot_general | solution.py:35
  138.2 0.0 all-gather.8.cloned.1.call-update
  138.3 80.2 %all-gather.8.cloned.1.call-done = bf16[4096,1536]{1,0:T(8,128)(2,1)} async-done(((bf16[1024,1536]{1,0:T(8,128)(2,1)}), bf16[4096,1536]{1,0:T(8,128)(2,1)}) %all-gather.8.cloned.1.call-update) | async-done | bytes 12582928 | tf_op jit(solution)/shard_map/all_gather | solution.py:41
  218.5 19.7 %fusion.8 = f32[1,1024,1536]{1,2,0:T(8,128)} fusion(bf16[4096,1536]{1,0:T(8,128)(2,1)} %all-gather.8.cloned.1.call-done, bf16[1,1024,4096]{2,1,0:T(8,128)(2,1)} %param.11), kind=kOutput, calls=%fused_computation.9 | convolution fusion | flops 12884901888 | bytes 27262976 | tf_op jit(solution)/shard_map/dot_general | solution.py:42
  238.2 6.6 %copy.12 = f32[1,1024,1536]{2,1,0:T(8,128)} copy(f32[1,1024,1536]{1,2,0:T(8,128)} %fusion.8) | data formatting | bytes 12582912 | tf_op jit(solution)/shard_map/broadcast_in_dim | solution.py:43
  (4 shorter events, 0.1 us)
Async XLA Ops:
  6.5 51.6 %copy-start = (bf16[1,192,4096]{2,1,0:T(8,128)(2,1)S(1)}, bf16[1,192,4096]{2,1,0:T(8,128)(2,1)}, u32[]{:S(2)}) copy-start(bf16[1,192,4096]{2,1,0:T(8,128)(2,1)} %param.7) | copy-start | bytes 4718596
  6.5 94.7 %all-gather.4.cloned.1.call-start = ((), (), s32[]{:S(2)}) async-start(), calls=%async_computation.2 | async-start | bytes 2949120 | tf_op jit(solution)/shard_map/all_gather | solution.py:18
  9.3 114.8 %all-gather.6.cloned.1.call-start = ((), (), s32[]{:S(2)}) async-start(), calls=%async_computation.3 | async-start | bytes 8847360 | tf_op jit(solution)/shard_map/all_gather | solution.py:37
  60.9 40.3 %all-to-all-start = ((bf16[192,4,1024]{2,0,1:T(8,128)(2,1)}), bf16[192,4,1024]{2,0,1:T(8,128)(2,1)S(1)}, u32[]{:S(2)}, u32[]{:S(2)}) async-start(bf16[192,4,1024]{2,0,1:T(8,128)(2,1)} %copy.11), calls=%async_computation | async-start | bytes 3145728 | tf_op jit(solution)/shard_map/all_to_all | solution.py:15
  64.5 153.9 %all-gather.8.cloned.1.call-start = ((), (), s32[]{:S(2)}) async-start(), calls=%async_computation.4 | async-start | bytes 15728640 | tf_op jit(solution)/shard_map/all_gather | solution.py:41
  101.2 1.1 copy-start.1
Sparse Core Ops, SparseCore 0:
  9.5 26.7 all-gather.3
  58.2 65.8 all-gather.5
  138.4 80.0 all-gather.7
where the time goes:
time: 252 us; the launch traced here: 251 us
  waiting for transfers between devices  124 us (49%)
  blocking collectives  48.7 us (19%)
  matrix products  38.6 us (15%)
  local copies, waits for them, and re-layouts  19.5 us (8%)
  between operations  13.9 us (6%)
  starting transfers between devices  3.7 us (1%)
  other arithmetic  3.08 us (1%)
    all_gather x1, waiting for transfers between devices, shards(): everything = lax.all_gather(weighted, 'blk', axis=0, tiled=True)  80.2 us
    all_to_all x1, blocking collectives, shards(): lax.all_to_all(left_rows, 'expert', split_axis=0, concat_axis=1, tiled=True)  48.7 us
    all_to_all x1, waiting for transfers between devices, shards(): lax.all_to_all(grad_rows, 'blk', split_axis=1, concat_axis=0, tiled=True)  34.6 us
    dot_general x1, matrix products, shards(): jnp.dot(inverse_rows, everything, preferred_element_type=jnp.float32)  19.7 us
    dot_general x1, matrix products, shards(): jnp.dot(picked, lax.all_gather(arrived, 'blk', axis=2, tiled=True)[0], pr...  14.1 us
    all_gather x1, waiting for transfers between devices, shards(): lax.all_gather(arrived, 'blk', axis=2, tiled=True)[0]  8.9 us
    gather x1, local copies, waits for them, and re-layouts, shards(): jnp.take(gradient, row_index, axis=1)  8.06 us
    broadcast_in_dim x1, local copies, waits for them, and re-layouts, shards(): return result[None]  6.56 us
  transfers between devices with their start and end apart: 4, of which 3 were waited for; matrix products, arithmetic and copies ran while one was open for 7% of the time, Pallas kernels for 0%

commit v1 on v0

v1 whole, which is shorter than its diff:
```python
import jax
import jax.numpy as jnp
from jax import lax
from jax.sharding import PartitionSpec as P


def shards(inputs, output_grads, route_counts, left_rows, left_lengths, right_inverse):
    token_rows = inputs[0]
    slot_count, width_in = token_rows.shape
    owners, piece_slots = left_lengths.shape[1], left_rows.shape[1]
    live_rows = lax.broadcasted_iota(jnp.int32, (slot_count, 1), 0) < route_counts[0, 0]
    masked = jnp.where(live_rows, token_rows, jnp.zeros_like(token_rows))
    tokens = lax.all_gather(masked, "blk", axis=0, tiled=True)
    grads = lax.all_gather(output_grads[0], "blk", axis=0, tiled=True)
    arrived = lax.all_to_all(left_rows, "expert", split_axis=0, concat_axis=1, tiled=True)[0]

    lengths = lax.dynamic_index_in_dim(left_lengths, lax.axis_index("expert"), 0, keepdims=False)
    starts = jnp.cumsum(lengths) - lengths
    offset = lax.broadcasted_iota(jnp.int32, (owners, piece_slots), 1)
    row_index = jnp.where(offset < lengths[:, None], starts[:, None] + offset, -1)
    row_index = row_index.reshape(1, owners * piece_slots)
    select = lax.broadcasted_iota(jnp.int32, (width_in, 1), 0) == row_index
    picked = jnp.dot(tokens, select.astype(jnp.bfloat16), preferred_element_type=jnp.float32)
    picked = picked.astype(jnp.bfloat16)
    mixed = lax.dot_general(
        arrived, picked, (((0,), (1,)), ((), ())), preferred_element_type=jnp.float32
    ).astype(jnp.bfloat16)
    mixed = lax.all_gather(mixed, "blk", axis=0, tiled=True)

    trans_b = (((1,), (1,)), ((), ()))
    scores = lax.dot_general(
        right_inverse[0], grads, trans_b, preferred_element_type=jnp.float32
    ).astype(jnp.bfloat16)
    result = lax.dot_general(scores, mixed, trans_b, preferred_element_type=jnp.float32)
    return result[None]


def solution(mesh):
    in_specs = (
        P("expert", "blk", None),
        P("expert", "blk", None),
        P("expert", "blk"),
        P(None, "expert", "blk"),
        P(),
        P("expert", "blk", None),
    )
    out_specs = P("expert", "blk", None)
    return jax.shard_map(shards, mesh=mesh, in_specs=in_specs, out_specs=out_specs, check_vma=False)
```

time: 252 us -> 166 us (0.66)
  blocking collectives: 48.7 us -> 0 us
  local copies, waits for them, and re-layouts: 19.5 us -> 0.77 us
  waiting for transfers between devices: 124 us -> 111 us
  matrix products: 38.6 us -> 30 us
  starting transfers between devices: 3.7 us -> 7.4 us
    all_to_all x1 -> x0, blocking collectives: 48.7 us -> none  [shards(): lax.all_to_all(left_rows, 'expert', split_axis=0, concat_axis=1, tiled=True)]
    all_gather x3, waiting for transfers between devices: 89.1 us -> 70.4 us  [the longest x1 48 us: shards(): grads = lax.all_gather(output_grads[0], 'blk', axis=0, tiled=True)]
    dot_general x3 -> x2, matrix products: 38.6 us -> 30 us  [the longest x1 20 us: shards(): lax.dot_general(scores, mixed, trans_b, preferred_element_type=jnp.float32)]
    gather x1 -> x0, local copies, waits for them, and re-layouts: 8.06 us -> none  [shards(): jnp.take(gradient, row_index, axis=1)]
    broadcast_in_dim x1 -> x0, local copies, waits for them, and re-layouts: 6.56 us -> none  [shards(): return result[None]]
    all_to_all x1, waiting for transfers between devices: 34.6 us -> 39.4 us  [shards(): lax.all_to_all(left_rows, 'expert', split_axis=0, concat_axis=1, tiled=True)]
    all_to_all x1, starting transfers between devices: 3.61 us -> 7.32 us  [shards(): lax.all_to_all(left_rows, 'expert', split_axis=0, concat_axis=1, tiled=True)]
    all_to_all x2 -> x0, local copies, waits for them, and re-layouts: 2.8 us -> none  [shards(): lax.all_to_all(grad_rows, 'blk', split_axis=1, concat_axis=0, tiled=True)]
  transfers between devices with their start and end apart: 4 -> 4, of which waited for: 3 -> 3; matrix products, arithmetic and copies ran while one was open for 7% -> 1% of each run, Pallas kernels for 0% -> 0%
where the time goes in v1:
time: 166 us
  waiting for transfers between devices  111 us (67%)
  matrix products  30 us (18%)
  between operations  13.8 us (8%)
  starting transfers between devices  7.4 us (4%)
  other arithmetic  2.95 us (2%)
    all_gather x1, waiting for transfers between devices, shards(): grads = lax.all_gather(output_grads[0], 'blk', axis=0, tiled=True)  48 us
    all_to_all x1, waiting for transfers between devices, shards(): lax.all_to_all(left_rows, 'expert', split_axis=0, concat_axis=1, tiled=True)  39.4 us
    all_gather x1, waiting for transfers between devices, shards(): mixed = lax.all_gather(mixed, 'blk', axis=0, tiled=True)  22.5 us
    dot_general x1, matrix products, shards(): lax.dot_general(scores, mixed, trans_b, preferred_element_type=jnp.float32)  20 us
    dot_general x1, matrix products, shards(): lax.dot_general(arrived, picked, (((0,), (1,)), ((), ())), preferred_elem...  10 us
    all_to_all x1, starting transfers between devices, shards(): lax.all_to_all(left_rows, 'expert', split_axis=0, concat_axis=1, tiled=True)  7.32 us
  transfers between devices with their start and end apart: 4, of which 3 were waited for; matrix products, arithmetic and copies ran while one was open for 1% of the time, Pallas kernels for 0%

profile of v1, /device:TPU:0, one launch (start us, length us, event | category | flops | bytes accessed | tf_op | source)
XLA Modules:
  0.0 165.5 jit_solution(11271811725548098723)
XLA Ops:
  6.5 0.0 all-gather.5.cloned.1.call-start
  7.2 2.0 %bitcast_select_fusion = bf16[192,1536]{1,0:T(8,128)(2,1)} fusion(bf16[1,192,1536]{2,1,0:T(8,128)(2,1)} %param.6, pred[192]{0:T(512)(128)(4,1)S(1)} %iota_compare_fusion.7), kind=kLoop, calls=%fused_computation.11 | loop fusion | flops 294912 | bytes 1179840 | tf_op jit(solution)/shard_map/jit(_where)/select_n | solution.py:12
  9.2 0.0 all-gather.5.cloned.1.call-update
  9.2 7.3 %all-to-all-start = ((bf16[8,288,384]{2,1,0:T(8,128)(2,1)}), bf16[8,288,384]{2,1,0:T(8,128)(2,1)S(1)}, u32[]{:S(2)}, u32[]{:S(2)}) async-start(bf16[8,288,384]{2,1,0:T(8,128)(2,1)} %param.9), calls=%async_computation | async-start | bytes 3538944 | tf_op jit(solution)/shard_map/all_to_all | solution.py:15
  16.5 0.0 all-gather.7.cloned.1.call-start
  16.6 0.7 fusion.16
  17.3 0.2 reduce-window.8
  17.5 0.7 bitcast_subtract_fusion
  18.2 0.1 add_select_fusion
  18.2 0.1 select_n.22
  18.3 39.4 %all-to-all-done = bf16[8,288,384]{2,1,0:T(8,128)(2,1)S(1)} async-done(((bf16[8,288,384]{2,1,0:T(8,128)(2,1)}), bf16[8,288,384]{2,1,0:T(8,128)(2,1)S(1)}, u32[]{:S(2)}, u32[]{:S(2)}) %all-to-all-start) | async-done | bytes 1769504 | tf_op jit(solution)/shard_map/all_to_all | solution.py:15
  57.8 0.0 all-gather.5.cloned.1.call-done
  57.8 10.0 %fusion.15 = bf16[384,768]{0,1:T(8,128)(2,1)} fusion(bf16[2304,384]{1,0:T(8,128)(2,1)S(1)} %bitcast.33, bf16[768,1536]{1,0:T(8,128)(2,1)} %all-gather.5.cloned.1.call-done, s32[2304]{0:T(1024)S(1)} %select_n.22), kind=kOutput, calls=%fused_computation.10 | convolution fusion | flops 6800375808 | bytes 4727808 | tf_op jit(solution)/shard_map/dot_general | solution.py:25
  67.8 0.0 all-gather.7.cloned.1.call-update
  67.8 0.0 all-gather.9.cloned.1.call-start
  67.8 0.7 all-gather.9.cloned.1.call-update
  68.5 22.5 %all-gather.7.cloned.1.call-done = bf16[1536,768]{0,1:T(8,128)(2,1)} async-done(((bf16[384,768]{0,1:T(8,128)(2,1)}), bf16[1536,768]{0,1:T(8,128)(2,1)}) %all-gather.7.cloned.1.call-update) | async-done | bytes 2359312 | tf_op jit(solution)/shard_map/all_gather | solution.py:28
  91.0 48.0 %all-gather.9.cloned.1.call-done = bf16[1,768,4096]{2,1,0:T(8,128)(2,1)} async-done(((bf16[1,192,4096]{2,1,0:T(8,128)(2,1)}), bf16[1,768,4096]{2,1,0:T(8,128)(2,1)}) %all-gather.9.cloned.1.call-update) | async-done | bytes 6291472 | tf_op jit(solution)/shard_map/all_gather | solution.py:14
  139.0 20.0 %convolution_bitcast_fusion = f32[1,1024,1536]{2,1,0:T(8,128)} fusion(bf16[1536,768]{0,1:T(8,128)(2,1)} %all-gather.7.cloned.1.call-done, bf16[1,768,4096]{2,1,0:T(8,128)(2,1)} %all-gather.9.cloned.1.call-done, bf16[1,1024,4096]{2,1,0:T(8,128)(2,1)} %param.11), kind=kOutput, calls=%fused_computation.7 | convolution fusion | flops 8859156480 | bytes 23330816 | tf_op jit(solution)/shard_map/dot_general | solution.py:34
  (1 shorter events, 0.0 us)
Async XLA Ops:
  6.5 51.2 %all-gather.5.cloned.1.call-start = ((), (), s32[]{:S(2)}) async-start(), calls=%async_computation.1 | async-start | bytes 2949120 | tf_op jit(solution)/shard_map/all_gather | solution.py:13
  9.2 48.5 %all-to-all-start = ((bf16[8,288,384]{2,1,0:T(8,128)(2,1)}), bf16[8,288,384]{2,1,0:T(8,128)(2,1)S(1)}, u32[]{:S(2)}, u32[]{:S(2)}) async-start(bf16[8,288,384]{2,1,0:T(8,128)(2,1)} %param.9), calls=%async_computation | async-start | bytes 3538944 | tf_op jit(solution)/shard_map/all_to_all | solution.py:15
  16.5 74.5 %all-gather.7.cloned.1.call-start = ((), (), s32[]{:S(2)}) async-start(), calls=%async_computation.2 | async-start | bytes 2949120 | tf_op jit(solution)/shard_map/all_gather | solution.py:28
  67.8 71.2 %all-gather.9.cloned.1.call-start = ((), (), s32[]{:S(2)}) async-start(), calls=%async_computation.3 | async-start | bytes 7864320 | tf_op jit(solution)/shard_map/all_gather | solution.py:14
Sparse Core Ops, SparseCore 0:
  9.3 26.7 all-gather.4
  67.9 23.0 all-gather.6
  92.6 46.3 all-gather.8

commit v2 on v1

--- a/solution.py
+++ b/solution.py
@@ -1,7 +1,240 @@
+import functools
+
 import jax
 import jax.numpy as jnp
 from jax import lax
+from jax.experimental import pallas as pl
+from jax.experimental.pallas import tpu as pltpu
 from jax.sharding import PartitionSpec as P
+
+MESH = pl.DeviceIdType.MESH
+GRAD_PARTS = 4
+MIX_PARTS = 2
+
+
+def gather_kernel(
+    experts, group, x_ref, dy_ref, count_ref, pieces_ref, lengths_ref, right_ref,
+    scores_ref, mixed_ref,
+    x_own, x_all, dy_all, right, arrived, picked, mix_own, scores,
+    local_sem, send_sem, recv_sem,
+):
+    expert, block = lax.axis_index("expert"), lax.axis_index("blk")
+    mate = block + 1 - 2 * (block % 2)
+    across = (block + 2) % group
+    corner = (mate + 2) % group
+    slots, width_in = x_ref.shape
+    width_out = dy_ref.shape[1]
+    owners, piece, columns = pieces_ref.shape
+    tokens = slots * group
+    own_rows = right_ref.shape[0]
+
+    numbers = iter(range(1000))
+    local_numbers = iter(range(1000))
+
+    def rows_of(source, part=0, parts=1):
+        size = slots // parts
+        return pl.ds(pl.multiple_of(source * slots + part * size, 16), size)
+
+    def local(source, target):
+        copy = pltpu.make_async_copy(source, target, local_sem.at[next(local_numbers)])
+        copy.start()
+        return copy
+
+    def remote(source, target, number, device):
+        return pltpu.make_async_remote_copy(
+            src_ref=source, dst_ref=target, send_sem=send_sem.at[number],
+            recv_sem=recv_sem.at[number], device_id=device, device_id_type=MESH,
+        )
+
+    sent = []
+
+    def send(source, target, number, device):
+        copy = remote(source, target, number, device)
+        copy.start()
+        sent.append(copy)
+
+    def receive(target, number, device):
+        remote(target, target, number, device).wait_recv()
+
+    to_mate, to_across = (expert, mate), (expert, across)
+
+    x_load = local(x_ref, x_own)
+    dy_load = local(dy_ref, dy_all.at[rows_of(block)])
+    right_load = local(right_ref, right)
+    piece_rows = lambda owner: pl.ds(pl.multiple_of(owner * piece, 16), piece)
+    piece_load = local(pieces_ref.at[expert], arrived.at[piece_rows(expert)])
+
+    shifts = sorted(range(1, experts), key=lambda k: abs(k - experts / 2))
+    barrier = pltpu.get_barrier_semaphore()
+    for shift in shifts:
+        pl.semaphore_signal(
+            barrier, inc=1, device_id=((expert + shift) % experts, block), device_id_type=MESH
+        )
+    for device in (to_mate, to_across):
+        pl.semaphore_signal(barrier, inc=1, device_id=device, device_id_type=MESH)
+    pl.semaphore_wait(barrier, experts + 1)
+
+    piece_numbers = []
+    for shift in shifts:
+        number = next(numbers)
+        piece_numbers.append(number)
+        target = (expert + shift) % experts
+        send(pieces_ref.at[target], arrived.at[piece_rows(expert)], number, (target, block))
+
+    x_load.wait()
+    live = lax.broadcasted_iota(jnp.int32, (slots, 1), 0) < count_ref[0, 0]
+    x_all[rows_of(block), :] = jnp.where(
+        live, x_own[...].astype(jnp.float32), 0.0
+    ).astype(jnp.bfloat16)
+    x_mate, x_across, x_pass = next(numbers), next(numbers), next(numbers)
+    own = x_all.at[rows_of(block)]
+    send(own, own, x_across, to_across)
+    send(own, own, x_mate, to_mate)
+
+    dy_mate = next(numbers)
+    dy_across = [next(numbers) for _ in range(GRAD_PARTS)]
+    dy_pass = [next(numbers) for _ in range(GRAD_PARTS)]
+    for part, number in enumerate(dy_across):
+        size = slots // GRAD_PARTS
+        send(
+            dy_ref.at[pl.ds(part * size, size)],
+            dy_all.at[rows_of(block, part, GRAD_PARTS)], number, to_across,
+        )
+    send(dy_ref, dy_all.at[rows_of(block)], dy_mate, to_mate)
+
+    receive(x_all.at[rows_of(across)], x_across, to_across)
+    send(x_all.at[rows_of(across)], x_all.at[rows_of(across)], x_pass, to_mate)
+    receive(x_all.at[rows_of(mate)], x_mate, to_mate)
+
+    trans_b = (((1,), (1,)), ((), ()))
+    pair_width = 2 * slots
+    tile = min(256, own_rows)
+
+    def score(pair):
+        rows = pl.ds(pl.multiple_of(pair * pair_width, 128), pair_width)
+
+        @pl.loop(0, own_rows // tile)
+        def _(step):
+            here = pl.ds(pl.multiple_of(step * tile, tile), tile)
+            scores[here, rows] = lax.dot_general(
+                right[here, :], dy_all[rows, :], trans_b, preferred_element_type=jnp.float32
+            ).astype(jnp.bfloat16)
+
+    receive(x_all.at[rows_of(corner)], x_pass, to_mate)
+
+    lengths = [lengths_ref[expert, i] for i in range(owners)]
+    starts = [jnp.int32(0)]
+    for length in lengths[:-1]:
+        starts.append(starts[-1] + length)
+    wide = 256
+
+    @pl.loop(0, owners * piece // wide)
+    def _(step):
+        slot = lax.broadcasted_iota(jnp.int32, (1, wide), 1) + step * wide
+        index = jnp.full((1, wide), -1, jnp.int32)
+        for i in range(owners):
+            offset = slot - i * piece
+            index = jnp.where((offset >= 0) & (offset < lengths[i]), starts[i] + offset, index)
+        select = lax.broadcasted_iota(jnp.int32, (width_in, wide), 0) == index
+        select = jnp.where(select, 1.0, 0.0).astype(jnp.bfloat16)
+        picked[:, pl.ds(pl.multiple_of(step * wide, wide), wide)] = jnp.dot(
+            x_all[...], select, preferred_element_type=jnp.float32
+        ).astype(jnp.bfloat16)
+
+    dy_load.wait()
+    right_load.wait()
+    receive(dy_all.at[rows_of(mate)], dy_mate, to_mate)
+    score(block // 2)
+
+    def pass_grads(part):
+        here = dy_all.at[rows_of(across, part, GRAD_PARTS)]
+        receive(here, dy_across[part], to_across)
+        send(here, here, dy_pass[part], to_mate)
+
+    for part in range(GRAD_PARTS - 1):
+        pass_grads(part)
+
+    piece_load.wait()
+    for shift, number in zip(shifts, piece_numbers):
+        source = (expert + experts - shift) % experts
+        receive(arrived.at[piece_rows(source)], number, (source, block))
+
+    mix_size = tokens // MIX_PARTS
+    mix_mate = [next(numbers) for _ in range(MIX_PARTS)]
+    mix_across = [next(numbers) for _ in range(MIX_PARTS)]
+    mix_pass = [next(numbers) for _ in range(MIX_PARTS)]
+    mix_keep = []
+
+    def mix_at(source, part):
+        lanes = pl.ds(pl.multiple_of(source * columns, 128), columns)
+        return mixed_ref.at[pl.ds(part * mix_size, mix_size), lanes]
+
+    for part in range(MIX_PARTS):
+        here = pl.ds(part * mix_size, mix_size)
+        mix_own[here, :] = jnp.dot(
+            picked[here, :], arrived[...], preferred_element_type=jnp.float32
+        ).astype(jnp.bfloat16)
+        send(mix_own.at[here], mix_at(block, part), mix_across[part], to_across)
+        send(mix_own.at[here], mix_at(block, part), mix_mate[part], to_mate)
+        mix_keep.append(local(mix_own.at[here], mix_at(block, part)))
+
+    pass_grads(GRAD_PARTS - 1)
+    for part in range(GRAD_PARTS):
+        receive(dy_all.at[rows_of(corner, part, GRAD_PARTS)], dy_pass[part], to_mate)
+    score(1 - block // 2)
+    scores_keep = local(scores, scores_ref)
+
+    for part in range(MIX_PARTS):
+        receive(mix_at(across, part), mix_across[part], to_across)
+        send(mix_at(across, part), mix_at(across, part), mix_pass[part], to_mate)
+    for part in range(MIX_PARTS):
+        receive(mix_at(mate, part), mix_mate[part], to_mate)
+    for part in range(MIX_PARTS):
+        receive(mix_at(corner, part), mix_pass[part], to_mate)
+    for copy in mix_keep:
+        copy.wait()
+    scores_keep.wait()
+    for copy in sent:
+        copy.wait_send()
+
+
+def paired(experts, group, inputs, output_grads, route_counts, left_rows, left_lengths, right_inverse):
+    slots, width_in = inputs.shape[1:]
+    width_out = output_grads.shape[2]
+    owners, piece, columns = left_rows.shape
+    own_rows = right_inverse.shape[1]
+    tokens = group * slots
+    copies = experts - 1 + 4 + 2 * GRAD_PARTS + 3 * MIX_PARTS
+    any_space = pl.BlockSpec(memory_space=pl.ANY)
+    scalars = pl.BlockSpec(memory_space=pltpu.SMEM)
+    bf16 = jnp.bfloat16
+    scores, mixed = pl.pallas_call(
+        functools.partial(gather_kernel, experts, group),
+        name="exchange",
+        out_shape=(
+            jax.ShapeDtypeStruct((own_rows, tokens), bf16),
+            jax.ShapeDtypeStruct((tokens, width_in), bf16),
+        ),
+        in_specs=[any_space, any_space, scalars, any_space, scalars, any_space],
+        out_specs=(any_space, any_space),
+        scratch_shapes=[
+            pltpu.VMEM((slots, width_in), bf16),
+            pltpu.VMEM((tokens, width_in), bf16),
+            pltpu.VMEM((tokens, width_out), bf16),
+            pltpu.VMEM((own_rows, width_out), bf16),
+            pltpu.VMEM((owners * piece, columns), bf16),
+            pltpu.VMEM((tokens, owners * piece), bf16),
+            pltpu.VMEM((tokens, columns), bf16),
+            pltpu.VMEM((own_rows, tokens), bf16),
+            pltpu.SemaphoreType.DMA((5 + MIX_PARTS,)),
+            pltpu.SemaphoreType.DMA((copies,)),
+            pltpu.SemaphoreType.DMA((copies,)),
+        ],
+        compiler_params=pltpu.CompilerParams(
+            collective_id=0, has_side_effects=True, vmem_limit_bytes=60 * 2**20
+        ),
+    )(inputs[0], output_grads[0], route_counts, left_rows, left_lengths, right_inverse[0])
+    return jnp.dot(scores, mixed, preferred_element_type=jnp.float32)[None]
 
 
 def shards(inputs, output_grads, route_counts, left_rows, left_lengths, right_inverse):
@@ -45,4 +278,6 @@
         P("expert", "blk", None),
     )
     out_specs = P("expert", "blk", None)
-    return jax.shard_map(shards, mesh=mesh, in_specs=in_specs, out_specs=out_specs, check_vma=False)
+    experts, group = mesh.shape["expert"], mesh.shape["blk"]
+    step = functools.partial(paired, experts, group) if group == 4 else shards
+    return jax.shard_map(step, mesh=mesh, in_specs=in_specs, out_specs=out_specs, check_vma=False)

time: 166 us -> 78.3 us (0.47)
  waiting for transfers between devices: 111 us -> 0 us
  Pallas kernels: 0 us -> 70 us
  matrix products: 30 us -> 7.45 us
  between operations: 13.8 us -> 0.66 us
  starting transfers between devices: 7.4 us -> 0 us
  other arithmetic: 2.95 us -> 0 us
    all_gather x3 -> x0, waiting for transfers between devices: 70.4 us -> none  [the longest x1 48 us: shards(): grads = lax.all_gather(output_grads[0], 'blk', axis=0, tiled=True)]
    pallas_call x0 -> x1, Pallas kernels: none -> 70 us  [paired(): pl.pallas_call(functools.partial(gather_kernel, experts, group), name='ex...]
    all_to_all x1 -> x0, waiting for transfers between devices: 39.4 us -> none  [shards(): lax.all_to_all(left_rows, 'expert', split_axis=0, concat_axis=1, tiled=True)]
    dot_general x2 -> x1, matrix products: 30 us -> 7.45 us  [paired(): return jnp.dot(scores, mixed, preferred_element_type=jnp.float32)[None]]
    all_to_all x1 -> x0, starting transfers between devices: 7.32 us -> none  [shards(): lax.all_to_all(left_rows, 'expert', split_axis=0, concat_axis=1, tiled=True)]
    select_n x2 -> x0, other arithmetic: 2.07 us -> none  [the longest x1 1.99 us: shards(): masked = jnp.where(live_rows, token_rows, jnp.zeros_like(token_rows))]
  transfers between devices with their start and end apart: 4 -> 0, of which waited for: 3 -> 0; matrix products, arithmetic and copies ran while one was open for 1% -> 0% of each run, Pallas kernels for 0% -> 0%
where the time goes in v2:
time: 78.3 us; the launch traced here: 78.1 us
  Pallas kernels  70 us (89%)
  matrix products  7.45 us (10%)
    pallas_call x1, Pallas kernels, paired(): pl.pallas_call(functools.partial(gather_kernel, experts, group), name='ex...  70 us
    dot_general x1, matrix products, paired(): return jnp.dot(scores, mixed, preferred_element_type=jnp.float32)[None]  7.45 us

profile of v2, /device:TPU:0, one launch (start us, length us, event | category | flops | bytes accessed | tf_op | source)
XLA Modules:
  0.0 78.1 jit_solution(7283058839851470425)
XLA Ops:
  0.7 70.0 %exchange.1 = (bf16[1024,768]{1,0:T(8,128)(2,1)}, bf16[768,1536]{1,0:T(8,128)(2,1)}) custom-call(bf16[192,1536]{1,0:T(8,128)(2,1)} %bitcast.9, bf16[192,4096]{1,0:T(8,128)(2,1)} %bitcast.8, s32[1,1]{1,0:T(1,128)S(6)} %copy.7.count_ref, bf16[8,288,384]{2,1,0:T(8,128)(2,1)} %pieces_ref.1, s32[8,8]{1,0:T(8,128)} %lengths_ref.1, bf16[1024,4096]{1,0:T(8,128)(2,1)} %bitcast.7), custom_call_target="tpu_custom_call" | custom-call | tf_op jit(solution)/shard_map/exchange/pallas_call | solution.py:211
  70.6 7.4 %convolution_bitcast_fusion = f32[1,1024,1536]{2,1,0:T(8,128)} fusion(bf16[1024,768]{1,0:T(8,128)(2,1)} %get-tuple-element.7, bf16[768,1536]{1,0:T(8,128)(2,1)} %get-tuple-element.8), kind=kOutput, calls=%fused_computation | convolution fusion | flops 2415919104 | bytes 10223616 | tf_op jit(solution)/shard_map/dot_general | solution.py:237
